TPU v7x, 128 devices: a whole 4x4x4 slice. The times are simulated.
128 devices in a mesh: expert: 16 (over z_hi, x, core), dp: 8 (over z_lo, y).
Axes of the slice: x: 4, y: 4, z: 4 (z_hi: 2, z_lo: 2; z = z_hi * 2 + z_lo), core: 2. Of those that a mesh axis runs over, the one named last changes fastest.
Arguments:
- trunk: bfloat16 [3072, 4096], P(('dp', 'expert')), may hold values from -6 to 6
- w_first: bfloat16 [16, 4096, 2048], P('expert'), may hold values from -0.09375 to 0.09375
- w_second: bfloat16 [16, 2048, 1024], P('expert'), may hold values from -0.125 to 0.125
- gates: bfloat16 [16, 8, 3072], P('expert', None, 'dp'), may hold values from 0.049804688 to 1
- d_mixed: bfloat16 [3072, 8, 1024], P(('dp', 'expert')), may hold values from -6 to 6
Outputs:
- mixed: bfloat16 [3072, 8, 1024], P(('dp', 'expert'))
- d_trunk: bfloat16 [3072, 4096], P(('dp', 'expert'))
- d_gates: bfloat16 [16, 8, 3072], P('expert', None, 'dp')
- d_w_first: bfloat16 [16, 4096, 2048], P('expert', 'dp')
- d_w_second: bfloat16 [16, 2048, 1024], P('expert', 'dp')
All inputs are finite; a program needn't handle non-finite values.
Results may differ from a plain program's by a relative error of at most 0.015.
Values may be sent and summed in bfloat16 or wider, within the bound.
No kernel may reach another device: no remote copies, remote signals or barrier semaphores. Data moves between devices by JAX's collectives and lax.ppermute only.
A program may use at most 128 MiB of HBM per device.

v0:
```python
import jax
import jax.numpy as jnp
from jax import lax
from jax.experimental import pallas as pl
from jax.experimental.pallas import tpu as pltpu
from jax.sharding import PartitionSpec as P

AXES = ("expert", "dp")
BF = jnp.bfloat16
F32 = jnp.float32


def coords(i):
    e, d = divmod(i, 8)
    zl, y = divmod(d, 4)
    zh, r = divmod(e, 8)
    x, c = divmod(r, 2)
    return x, y, zh, zl, c


def index(x, y, zh, zl, c):
    return (zh * 8 + x * 2 + c) * 8 + zl * 4 + y


def swap(v, y=0, z=0, c=0):
    pairs = []
    for i in range(128):
        px, py, pzh, pzl, pc = coords(i)
        pairs.append((i, index(px, py ^ y, pzh ^ (z >> 1), pzl ^ (z & 1), pc ^ c)))
    return lax.ppermute(v, AXES, pairs)


def swap_split(v, k, first):
    pairs = []
    for i in range(128):
        px, py, pzh, pzl, pc = coords(i)
        if (pc == 0) == first:
            pzh, pzl = pzh ^ (k & 1), pzl ^ (k >> 1)
        else:
            px = px ^ k
        pairs.append((i, index(px, py, pzh, pzl, pc)))
    return lax.ppermute(v, AXES, pairs)


def after(v, *others):
    return lax.optimization_barrier((v,) + others)[0]


def grid():
    return [[coords(i), i] for i in range(128)]


def groups(key, order):
    rows = {}
    for at, i in grid():
        rows.setdefault(key(*at), []).append((order(*at), i))
    return [[i for _, i in sorted(rows[k])] for k in sorted(rows)]


PLANE = groups(lambda x, y, zh, zl, c: (y, c), lambda x, y, zh, zl, c: (x, zl, zh))
RING = groups(lambda x, y, zh, zl, c: (x, zh, zl, c), lambda x, y, zh, zl, c: y)


def exchange(v, members):
    return lax.all_to_all(v, AXES, 0, 0, axis_index_groups=members, tiled=True)


def dot(a, b, dims):
    return lax.dot_general(a, b, (dims, ((), ())), preferred_element_type=F32)


def pick(a, i, axis):
    return lax.dynamic_index_in_dim(a, i, axis, keepdims=False)


def place_kernel(at, *refs):
    out = refs[4]
    for i in range(16):
        out[at[i]] = refs[i // 4][i % 4]


def place(at, lines):
    return pl.pallas_call(
        place_kernel,
        out_shape=jax.ShapeDtypeStruct((16,) + lines[0].shape[1:], lines[0].dtype),
        in_specs=[pl.BlockSpec(memory_space=pltpu.SMEM)]
        + [pl.BlockSpec(memory_space=pltpu.VMEM)] * 4,
        out_specs=pl.BlockSpec(memory_space=pltpu.VMEM),
        compiler_params=pltpu.CompilerParams(vmem_limit_bytes=16 << 20),
        cost_estimate=pl.CostEstimate(flops=0, bytes_accessed=6 << 20, transcendentals=0),
    )(at, *lines)


def gather(v, members):
    return exchange(jnp.broadcast_to(v[None], (len(members[0]),) + v.shape), members)


def on_device(trunk, w_first, w_second, gates, d_mixed):
    e = lax.axis_index("expert")
    d = lax.axis_index("dp")
    zl, y = d // 4, d % 4
    zh, x, c = e // 8, (e % 8) // 2, e % 2
    zz = zl * 2 + zh

    gate_rows = lax.all_to_all(
        gates[0].reshape(8, 16, 24).transpose(1, 0, 2), "expert", 0, 0, tiled=True
    )

    line = jnp.stack([trunk] + [swap_split(trunk, k, True) for k in (1, 2, 3)])
    far = [swap_split(line, k, False) for k in (2, 1, 3)]
    dx, dz = x ^ (jnp.arange(16) // 4), zz ^ (jnp.arange(16) % 4)
    ex, ez = x ^ (jnp.arange(16) % 4), zz ^ (jnp.arange(16) // 4)
    at = jnp.where(c == 0, dx * 4 + dz, ex * 4 + ez).astype(jnp.int32)
    own = place(at, [line, far[1], far[0], far[2]]).reshape(384, 4096)

    d_out_each = jnp.einsum(
        "etr,rto->ero", gate_rows, d_mixed, preferred_element_type=F32
    ).astype(BF)
    back = lax.all_to_all(d_out_each, "expert", 0, 0, tiled=True)

    half = lax.dynamic_slice_in_dim(w_first[0], zl * 1024, 1024, 1)
    cols = trunk.reshape(24, 2, 4, 512)
    t_y = [pick(cols, y ^ k, 2).reshape(24, 1024) for k in range(4)]
    t_y = jnp.stack([t_y[0]] + [swap(t_y[k], y=k) for k in (1, 3, 2)])

    own, back, half, t_y = lax.optimization_barrier((own, back, half, t_y))
    other = swap(own, c=1)
    back = back.reshape(2, 4, 2, 24, 1024)
    back_z = swap(back, z=1)
    wide = gather(t_y, PLANE).reshape(16, 4, 24, 1024)
    second = w_second[0]
    second_own = lax.dynamic_slice_in_dim(second, zl * 1024, 1024, 0)
    second_far = lax.dynamic_slice_in_dim(second, (1 - zl) * 1024, 1024, 0)

    def forward(rows):
        pre = dot(rows, half, ((1,), (0,)))
        sig = jax.nn.sigmoid(pre)
        slope = sig * (1.0 + pre * (1.0 - sig))
        return (pre * sig).astype(BF), slope

    def backward(d_o, slope):
        d_hidden = dot(d_o, second_own, ((1,), (1,)))
        return (d_hidden * slope).astype(BF)

    hidden_own, slope_own = forward(own)
    hidden_own, back_z, other = lax.optimization_barrier((hidden_own, back_z, other))
    pair = jnp.where(zl == 0, jnp.stack([back, back_z]), jnp.stack([back_z, back]))
    pair = pair.transpose(3, 2, 0, 1, 4, 5)
    d_output = jnp.where(c == 0, pair, pair[::-1]).reshape(768, 1024)

    d_own = backward(d_output[:384], slope_own)
    near_own = (swap(d_own, y=1), swap(d_own, y=3))
    hidden_other, slope_other = forward(other)
    d_other = backward(d_output[384:], slope_other)
    near_other = (swap(d_other, y=1), swap(d_other, y=3))

    d_other_late, *near_own = lax.optimization_barrier((d_other, *near_own))
    dt_other = dot(d_other_late, half, ((1,), (1,))).astype(BF)
    far_own = swap(near_own[1], y=1)
    hidden = jnp.concatenate([hidden_own, hidden_other])
    d_own_late, *near_other = lax.optimization_barrier((d_own, *near_other))
    dt = dot(d_own_late, half, ((1,), (1,))) + swap(dt_other, c=1).astype(F32)
    dt = dt.astype(BF)
    far_other = swap(near_other[0], y=3)

    ds = dot(hidden, d_output, ((0,), (0,))).astype(BF)
    d_second = lax.psum_scatter(
        ds, AXES, axis_index_groups=RING, scatter_dimension=0, tiled=True
    )

    by_z = hidden.reshape(8, 2, 48, 1024)
    mine = pick(by_z, zl, 1).reshape(384, 1024)
    theirs = swap(pick(by_z, 1 - zl, 1).reshape(384, 1024), z=1)
    output = dot(mine, second_own, ((1,), (0,))) + dot(theirs, second_far, ((1,), (0,)))
    output = output.astype(BF).reshape(2, 4, 2, 24, 1024)
    output = jnp.where(c == 0, output, output[::-1])
    output = output.transpose(2, 1, 0, 3, 4).reshape(16, 24, 1024)
    outs = lax.all_to_all(output, "expert", 0, 0, tiled=True)
    mixed = jnp.einsum(
        "etr,ero->rto", gate_rows, outs, preferred_element_type=F32
    ).astype(BF)
    d_gate = jnp.einsum(
        "rto,ero->etr", d_mixed, outs, preferred_element_type=F32
    ).astype(BF)

    dt = exchange(after(dt, outs).reshape(16, 24, 4096), PLANE)
    d_trunk = jnp.sum(dt, axis=0, dtype=F32).astype(BF)
    d_gate = lax.all_to_all(after(d_gate, dt), "expert", 0, 0, tiled=True)
    d_gate = d_gate.transpose(1, 0, 2).reshape(8, 384)

    wide = after(wide, *near_other)
    wide = wide.transpose(1, 0, 2, 3).reshape(1536, 1024)
    wide_other = swap(wide, c=1)
    tile = dot(wide[:1152], jnp.concatenate([d_own, *near_own]), ((0,), (0,)))
    tile = tile + dot(wide_other[:1152], jnp.concatenate([d_other, *near_other]), ((0,), (0,)))
    tile = tile + dot(wide[1152:], far_own, ((0,), (0,)))
    tile = tile + dot(wide_other[1152:], far_other, ((0,), (0,)))
    tile = tile.astype(BF).reshape(2, 512, 1024)
    far = swap(pick(tile, 1 - zl, 0), z=1)
    near = pick(tile, zl, 0)
    d_first = jnp.where(
        zl == 0,
        jnp.concatenate([near, far], axis=1),
        jnp.concatenate([far, near], axis=1),
    )
    return (mixed, d_trunk, d_gate[None], d_first[None], d_second[None])


def solution(mesh):
    in_specs = (
        P(("dp", "expert"), None),
        P("expert", None, None),
        P("expert", None, None),
        P("expert", None, "dp"),
        P(("dp", "expert"), None, None),
    )
    out_specs = (
        P(("dp", "expert"), None, None),
        P(("dp", "expert"), None),
        P("expert", None, "dp"),
        P("expert", "dp", None),
        P("expert", "dp", None),
    )
    return jax.shard_map(
        on_device, mesh=mesh, in_specs=in_specs, out_specs=out_specs, check_vma=False
    )
```

profile of v0, /device:TPU:1, one launch (start us, length us, event | category | flops | bytes accessed | tf_op | source)
XLA Modules:
  0.0 291.9 jit_solution(15985760292164382078)
XLA Ops:
  7.2 3.4 %collective-permute-start.2 = (bf16[24,4096]{1,0:T(8,128)(2,1)}, bf16[24,4096]{1,0:T(8,128)(2,1)S(1)}, u32[]{:S(2)}, u32[]{:S(2)}) collective-permute-start(bf16[24,4096]{1,0:T(8,128)(2,1)} %param.5), channel_id=1, source_target_pairs={{0,68},{1,69},{2,70},{3,71},{4,64},{5,65},{6,66},{7,67},{8,56},{9,... | collective-permute-start | bytes 589832 | tf_op jit(solution)/shard_map/ppermute | solution.py:42
  12.7 8.8 %all-to-all-start = ((bf16[16,8,24]{2,1,0:T(8,128)(2,1)}), bf16[16,8,24]{2,1,0:T(8,128)(2,1)S(1)}, u32[]{:S(2)}, u32[]{:S(2)}) async-start(bf16[16,8,24]{2,1,0:T(8,128)(2,1)} %copy.35), calls=%async_computation | async-start | bytes 65536 | tf_op jit(solution)/shard_map/all_to_all | solution.py:105
  31.4 7.8 %all-to-all-start.1 = ((bf16[16,24,1024]{2,1,0:T(8,128)(2,1)}), bf16[16,24,1024]{2,1,0:T(8,128)(2,1)}, u32[]{:S(2)}, u32[]{:S(2)}) async-start(bf16[16,24,1024]{2,1,0:T(8,128)(2,1)} %copy.37), calls=%async_computation.1 | async-start | bytes 1572864 | tf_op jit(solution)/shard_map/all_to_all | solution.py:119
  44.0 7.7 %dynamic-slice_bitcast_fusion = bf16[4096,1024]{1,0:T(8,128)(2,1)} fusion(bf16[1,4096,2048]{2,1,0:T(8,128)(2,1)} %param.6, s32[]{:T(128)S(6)} %select_n.130), kind=kLoop, calls=%fused_computation | loop fusion | bytes 16777220 | tf_op jit(solution)/shard_map/dynamic_slice | solution.py:121
  60.4 7.3 %collective-permute-done.4.refs_2_ = bf16[4,24,4096]{2,1,0:T(8,128)(2,1)S(1)} collective-permute-done((bf16[4,24,4096]{2,1,0:T(8,128)(2,1)S(1)}, bf16[4,24,4096]{2,1,0:T(8,128)(2,1)S(1)}, u32[]{:S(2)}, u32[]{:S(2)}) %collective-permute-start.4) | collective-permute-done | bytes 786464 | tf_op jit(solution)/shard_map/ppermute | solution.py:42
  76.3 5.6 %all-to-all-start.5 = ((bf16[16,4,24,1024]{3,2,1,0:T(8,128)(2,1)}), bf16[16,4,24,1024]{3,2,1,0:T(8,128)(2,1)}, u32[]{:S(2)}, u32[]{:S(2)}) async-start(bf16[16,4,24,1024]{3,2,1,0:T(8,128)(2,1)} %broadcast_in_dim.4), calls=%async_computation.5 | async-start | bytes 6291456 | tf_op jit(solution)/shard_map/all_to_all | solution.py:65
  82.1 7.8 %multiply_convert_fusion.3 = (bf16[384,1024]{1,0:T(8,128)(2,1)}, f32[384,1024]{1,0:T(8,128)S(1)}) fusion(bf16[384,4096]{1,0:T(8,128)(2,1)S(1)} %bitcast.89, bf16[4096,1024]{1,0:T(8,128)(2,1)} %dynamic-slice_bitcast_fusion), kind=kOutput, calls=%fused_computation.40 | convolution fusion | flops 3223191552 | bytes 13893632 | tf_op jit(solution)/shard_map/dot_general | solution.py:69
  89.9 16.4 %collective-permute-done.9 = bf16[2,4,2,24,1024]{4,3,2,1,0:T(8,128)(2,1)} collective-permute-done((bf16[2,4,2,24,1024]{4,3,2,1,0:T(8,128)(2,1)}, bf16[2,4,2,24,1024]{4,3,2,1,0:T(8,128)(2,1)}, u32[]{:S(2)}, u32[]{:S(2)}) %collective-permute-start.9) | collective-permute-done | bytes 786464 | tf_op jit(solution)/shard_map/ppermute | solution.py:30
  114.5 5.5 %multiply_convert_fusion.2 = (bf16[384,1024]{1,0:T(8,128)(2,1)S(1)}, f32[384,1024]{1,0:T(8,128)S(1)}) fusion(bf16[384,4096]{1,0:T(8,128)(2,1)} %collective-permute-done.10, bf16[4096,1024]{1,0:T(8,128)(2,1)S(1)} %bitcast.94), kind=kOutput, calls=%fused_computation.38 | convolution fusion | flops 3223191552 | bytes 13893632 | tf_op jit(solution)/shard_map/dot_general | solution.py:69
  122.2 7.0 %collective-permute-done.14 = bf16[384,1024]{1,0:T(8,128)(2,1)S(1)} collective-permute-done((bf16[384,1024]{1,0:T(8,128)(2,1)S(1)}, bf16[384,1024]{1,0:T(8,128)(2,1)S(1)}, u32[]{:S(2)}, u32[]{:S(2)}) %collective-permute-start.14) | collective-permute-done | bytes 786464 | tf_op jit(solution)/shard_map/ppermute | solution.py:30
  130.6 6.2 %convolution_convert_fusion = bf16[384,4096]{1,0:T(8,128)(2,1)} fusion(bf16[384,1024]{1,0:T(8,128)(2,1)} %multiply_convert_fusion, bf16[4096,1024]{1,0:T(8,128)(2,1)S(1)} %bitcast.94), kind=kOutput, calls=%fused_computation.2 | convolution fusion | flops 3222798336 | bytes 12320768 | tf_op jit(solution)/shard_map/dot_general | solution.py:69
  136.8 3.2 %collective-permute-start.16 = (bf16[384,4096]{1,0:T(8,128)(2,1)}, bf16[384,4096]{1,0:T(8,128)(2,1)}, u32[]{:S(2)}, u32[]{:S(2)}) collective-permute-start(bf16[384,4096]{1,0:T(8,128)(2,1)} %convolution_convert_fusion), channel_id=1, source_target_pairs={{0,8},{1,9},{2,10},{3,11},{4,12},{5,13},{6,14},{7,15},{8,0},{9,1},... | collective-permute-start | bytes 9437192 | tf_op jit(solution)/shard_map/ppermute | solution.py:30
  147.5 11.9 %collective-permute-done.12 = bf16[384,1024]{1,0:T(8,128)(2,1)} collective-permute-done((bf16[384,1024]{1,0:T(8,128)(2,1)}, bf16[384,1024]{1,0:T(8,128)(2,1)}, u32[]{:S(2)}, u32[]{:S(2)}) %collective-permute-start.12) | collective-permute-done | bytes 786464 | tf_op jit(solution)/shard_map/ppermute | solution.py:30
  164.2 4.6 %convolution_convert_fusion.1 = bf16[1024,1024]{1,0:T(8,128)(2,1)} fusion(bf16[768,1024]{1,0:T(8,128)(2,1)S(1)} %bitcast.101, bf16[384,1024]{1,0:T(8,128)(2,1)} %copy-done.6, bf16[384,1024]{1,0:T(8,128)(2,1)} %get-tuple-element.24), kind=kOutput, calls=%fused_computation.28 | convolution fusion | flops 1614807040 | bytes 5242880 | tf_op jit(solution)/shard_map/dot_general | solution.py:69
  177.0 14.4 %all-to-all-start.2 = ((bf16[16,24,1024]{2,1,0:T(8,128)(2,1)}), bf16[16,24,1024]{2,1,0:T(8,128)(2,1)}, u32[]{:S(2)}, u32[]{:S(2)}) async-start(bf16[16,24,1024]{2,1,0:T(8,128)(2,1)} %bitcast.99), calls=%async_computation.2 | async-start | bytes 1572864 | tf_op jit(solution)/shard_map/all_to_all | solution.py:178
  193.0 11.0 %add_convert_fusion = bf16[384,4096]{1,0:T(8,128)(2,1)} fusion(bf16[384,4096]{1,0:T(8,128)(2,1)} %collective-permute-done.16, bf16[384,1024]{1,0:T(8,128)(2,1)S(1)} %copy-done.12, bf16[4096,1024]{1,0:T(8,128)(2,1)} %dynamic-slice_bitcast_fusion), kind=kOutput, calls=%fused_computation.1 | convolution fusion | flops 3225944064 | bytes 15466496 | tf_op jit(solution)/shard_map/dot_general | solution.py:69
  206.0 5.9 %all-to-all-start.3 = ((bf16[16,24,4096]{2,1,0:T(8,128)(2,1)}), bf16[16,24,4096]{2,1,0:T(8,128)(2,1)}, u32[]{:S(2)}, u32[]{:S(2)}) async-start(bf16[16,24,4096]{2,1,0:T(8,128)(2,1)} %bitcast.98), calls=%async_computation.3 | async-start | bytes 6291456 | tf_op jit(solution)/shard_map/all_to_all | solution.py:65
  211.9 5.2 %fusion.2 = f32[1024,1024]{1,0:T(8,128)S(1)} fusion(bf16[1152,1024]{1,0:T(8,128)(2,1)} %bitcast.100, bf16[384,1024]{1,0:T(8,128)(2,1)} %copy-done.14, bf16[384,1024]{1,0:T(8,128)(2,1)} %copy-done.13, bf16[384,1024]{1,0:T(8,128)(2,1)} %copy-done.11), kind=kOutput, calls=%fused_computation.7 | convolution fusion | flops 2422996992 | bytes 8912896 | tf_op jit(solution)/shard_map/dot_general | solution.py:69
  217.2 4.3 %collective-permute-done.18 = bf16[384,1024]{1,0:T(8,128)(2,1)} collective-permute-done((bf16[384,1024]{1,0:T(8,128)(2,1)}, bf16[384,1024]{1,0:T(8,128)(2,1)}, u32[]{:S(2)}, u32[]{:S(2)}) %collective-permute-start.18) | collective-permute-done | bytes 786464 | tf_op jit(solution)/shard_map/ppermute | solution.py:30
  223.9 5.2 %fusion = f32[1024,1024]{1,0:T(8,128)S(1)} fusion(bf16[1536,1024]{1,0:T(8,128)(2,1)} %collective-permute-done.17, bf16[384,1024]{1,0:T(8,128)(2,1)} %collective-permute-done.13, bf16[384,1024]{1,0:T(8,128)(2,1)} %collective-permute-done.12, bf16[384,1024]{1,0:T(8,128)(2,1)} %multiply_convert_fusion), kind=kOutput, calls=%fused_computation.5 | convolution fusion | flops 2422996992 | bytes 8912896 | tf_op jit(solution)/shard_map/dot_general | solution.py:69
  229.2 3.0 %add_convert_fusion.1 = bf16[1024,1024]{1,0:T(8,128)(2,1)S(1)} fusion(f32[1024,1024]{1,0:T(8,128)S(1)} %fusion.50, f32[1024,1024]{1,0:T(8,128)S(1)} %fusion.2, f32[1024,1024]{1,0:T(8,128)S(1)} %fusion, bf16[384,1024]{1,0:T(8,128)(2,1)} %collective-permute-done.19, bf16[1536,1024]{1,0:T(8,128)(2,1)} %collective-permute-done.17), kind=kOutput, calls=%fused_computation.3 | convolution fusion | flops 809500672 | bytes 16252928 | tf_op jit(solution)/shard_map/dot_general | solution.py:69
  238.4 30.9 %all-to-all-done.3 = bf16[16,24,4096]{2,1,0:T(8,128)(2,1)} async-done(((bf16[16,24,4096]{2,1,0:T(8,128)(2,1)}), bf16[16,24,4096]{2,1,0:T(8,128)(2,1)}, u32[]{:S(2)}, u32[]{:S(2)}) %all-to-all-start.3) | async-done | bytes 3145760 | tf_op jit(solution)/shard_map/all_to_all | solution.py:65
  270.9 5.3 %all-to-all-start.4 = ((bf16[16,8,24]{2,1,0:T(8,128)(2,1)}), bf16[16,8,24]{2,1,0:T(8,128)(2,1)}, u32[]{:S(2)}, u32[]{:S(2)}) async-start(bf16[16,8,24]{2,1,0:T(8,128)(2,1)} %copy.48), calls=%async_computation.4 | async-start | bytes 65536 | tf_op jit(solution)/shard_map/all_to_all | solution.py:188
  278.3 3.1 %reduce_sum.12 = bf16[24,4096]{1,0:T(8,128)(2,1)} reduce(bf16[16,24,4096]{2,1,0:T(8,128)(2,1)} %all-to-all-done.3, bf16[]{:T(256)} %constant.132.clone.1), dimensions={0}, to_apply=%region_0.1 | reduce | flops 1474560 | bytes 3342338 | tf_op jit(solution)/shard_map/reduce_sum | solution.py:187
  (119 shorter events, 85.9 us)
Async XLA Ops:
  7.2 32.0 %collective-permute-start.2 = (bf16[24,4096]{1,0:T(8,128)(2,1)}, bf16[24,4096]{1,0:T(8,128)(2,1)S(1)}, u32[]{:S(2)}, u32[]{:S(2)}) collective-permute-start(bf16[24,4096]{1,0:T(8,128)(2,1)} %param.5), channel_id=1, source_target_pairs={{0,68},{1,69},{2,70},{3,71},{4,64},{5,65},{6,66},{7,67},{8,56},{9,... | collective-permute-start | bytes 589832 | tf_op jit(solution)/shard_map/ppermute | solution.py:42
  10.6 28.6 %collective-permute-start.1 = (bf16[24,4096]{1,0:T(8,128)(2,1)}, bf16[24,4096]{1,0:T(8,128)(2,1)S(1)}, u32[]{:S(2)}, u32[]{:S(2)}) collective-permute-start(bf16[24,4096]{1,0:T(8,128)(2,1)} %param.5), channel_id=1, source_target_pairs={{0,4},{1,5},{2,6},{3,7},{4,0},{5,1},{6,2},{7,3},{8,40},{9,41},{10,... | collective-permute-start | bytes 589832 | tf_op jit(solution)/shard_map/ppermute | solution.py:42
  11.1 28.1 %collective-permute-start = (bf16[24,4096]{1,0:T(8,128)(2,1)}, bf16[24,4096]{1,0:T(8,128)(2,1)S(1)}, u32[]{:S(2)}, u32[]{:S(2)}) collective-permute-start(bf16[24,4096]{1,0:T(8,128)(2,1)} %param.5), channel_id=1, source_target_pairs={{0,64},{1,65},{2,66},{3,67},{4,68},{5,69},{6,70},{7,71},{8,24},{9,... | collective-permute-start | bytes 589832 | tf_op jit(solution)/shard_map/ppermute | solution.py:42
  25.2 27.9 %collective-permute-start.8 = (bf16[24,1024]{1,0:T(8,128)(2,1)}, bf16[24,1024]{1,0:T(8,128)(2,1)}, u32[]{:S(2)}, u32[]{:S(2)}) collective-permute-start(bf16[24,1024]{1,0:T(8,128)(2,1)} %bitcast.44), channel_id=1, source_target_pairs={{0,2},{1,3},{2,0},{3,1},{4,6},{5,7},{6,4},{7,5},{8,10},{9,11},{10,... | collective-permute-start | bytes 147464 | tf_op jit(solution)/shard_map/ppermute | solution.py:30
  28.7 25.8 %collective-permute-start.7 = (bf16[24,1024]{1,0:T(8,128)(2,1)}, bf16[24,1024]{1,0:T(8,128)(2,1)}, u32[]{:S(2)}, u32[]{:S(2)}) collective-permute-start(bf16[24,1024]{1,0:T(8,128)(2,1)} %bitcast.42), channel_id=1, source_target_pairs={{0,3},{1,2},{2,1},{3,0},{4,7},{5,6},{6,5},{7,4},{8,11},{9,10},{10,... | collective-permute-start | bytes 147464 | tf_op jit(solution)/shard_map/ppermute | solution.py:30
  31.4 39.8 %all-to-all-start.1 = ((bf16[16,24,1024]{2,1,0:T(8,128)(2,1)}), bf16[16,24,1024]{2,1,0:T(8,128)(2,1)}, u32[]{:S(2)}, u32[]{:S(2)}) async-start(bf16[16,24,1024]{2,1,0:T(8,128)(2,1)} %copy.37), calls=%async_computation.1 | async-start | bytes 1572864 | tf_op jit(solution)/shard_map/all_to_all | solution.py:119
  39.3 21.1 %collective-permute-start.3 = (bf16[4,24,4096]{2,1,0:T(8,128)(2,1)S(1)}, bf16[4,24,4096]{2,1,0:T(8,128)(2,1)S(1)}, u32[]{:S(2)}, u32[]{:S(2)}) collective-permute-start(bf16[4,24,4096]{2,1,0:T(8,128)(2,1)S(1)} %pad_maximum_fusion.1.refs_0_), channel_id=1, source_target_pairs={{0,16},{1,17},{2,18},{3,19},{4,20},{5,21},{6,22},{7,23},{8,72},{9,... | collective-permute-start | bytes 2359304 | tf_op jit(solution)/shard_map/ppermute | solution.py:42
  42.3 25.4 %collective-permute-start.4 = (bf16[4,24,4096]{2,1,0:T(8,128)(2,1)S(1)}, bf16[4,24,4096]{2,1,0:T(8,128)(2,1)S(1)}, u32[]{:S(2)}, u32[]{:S(2)}) collective-permute-start(bf16[4,24,4096]{2,1,0:T(8,128)(2,1)S(1)} %pad_maximum_fusion.1.refs_0_), channel_id=1, source_target_pairs={{0,32},{1,33},{2,34},{3,35},{4,36},{5,37},{6,38},{7,39},{8,12},{9,... | collective-permute-start | bytes 2359304 | tf_op jit(solution)/shard_map/ppermute | solution.py:42
  44.0 24.7 %collective-permute-start.5 = (bf16[4,24,4096]{2,1,0:T(8,128)(2,1)S(1)}, bf16[4,24,4096]{2,1,0:T(8,128)(2,1)S(1)}, u32[]{:S(2)}, u32[]{:S(2)}) collective-permute-start(bf16[4,24,4096]{2,1,0:T(8,128)(2,1)S(1)} %pad_maximum_fusion.1.refs_0_), channel_id=1, source_target_pairs={{0,48},{1,49},{2,50},{3,51},{4,52},{5,53},{6,54},{7,55},{8,76},{9,... | collective-permute-start | bytes 2359304 | tf_op jit(solution)/shard_map/ppermute | solution.py:42
  71.2 35.2 %collective-permute-start.10 = (bf16[384,4096]{1,0:T(8,128)(2,1)}, bf16[384,4096]{1,0:T(8,128)(2,1)}, u32[]{:S(2)}, u32[]{:S(2)}) collective-permute-start(bf16[384,4096]{1,0:T(8,128)(2,1)} %bitcast.88), channel_id=1, source_target_pairs={{0,8},{1,9},{2,10},{3,11},{4,12},{5,13},{6,14},{7,15},{8,0},{9,1},... | collective-permute-start | bytes 9437192 | tf_op jit(solution)/shard_map/ppermute | solution.py:30
  71.6 34.8 %collective-permute-start.9 = (bf16[2,4,2,24,1024]{4,3,2,1,0:T(8,128)(2,1)}, bf16[2,4,2,24,1024]{4,3,2,1,0:T(8,128)(2,1)}, u32[]{:S(2)}, u32[]{:S(2)}) collective-permute-start(bf16[2,4,2,24,1024]{4,3,2,1,0:T(8,128)(2,1)} %bitcast.11), channel_id=1, source_target_pairs={{0,4},{1,5},{2,6},{3,7},{4,0},{5,1},{6,2},{7,3},{8,12},{9,13},{10,... | collective-permute-start | bytes 2359304 | tf_op jit(solution)/shard_map/ppermute | solution.py:30
  76.3 84.2 %all-to-all-start.5 = ((bf16[16,4,24,1024]{3,2,1,0:T(8,128)(2,1)}), bf16[16,4,24,1024]{3,2,1,0:T(8,128)(2,1)}, u32[]{:S(2)}, u32[]{:S(2)}) async-start(bf16[16,4,24,1024]{3,2,1,0:T(8,128)(2,1)} %broadcast_in_dim.4), calls=%async_computation.5 | async-start | bytes 6291456 | tf_op jit(solution)/shard_map/all_to_all | solution.py:65
  81.9 203.2 %reduce-scatter.2.cloned.1.call-start = ((), (), s32[]{:S(2)}) async-start(), calls=%async_computation.7 | async-start | bytes 2621440 | tf_op jit(solution)/shard_map/reduce_scatter | solution.py:167
  112.5 18.1 %collective-permute-start.15 = (bf16[384,1024]{1,0:T(8,128)(2,1)S(1)}, bf16[384,1024]{1,0:T(8,128)(2,1)S(1)}, u32[]{:S(2)}, u32[]{:S(2)}) collective-permute-start(bf16[384,1024]{1,0:T(8,128)(2,1)S(1)} %multiply_convert_fusion.1), channel_id=1, source_target_pairs={{0,3},{1,2},{2,1},{3,0},{4,7},{5,6},{6,5},{7,4},{8,11},{9,10},{10,... | collective-permute-start | bytes 2359304 | tf_op jit(solution)/shard_map/ppermute | solution.py:30
  136.8 56.2 %collective-permute-start.16 = (bf16[384,4096]{1,0:T(8,128)(2,1)}, bf16[384,4096]{1,0:T(8,128)(2,1)}, u32[]{:S(2)}, u32[]{:S(2)}) collective-permute-start(bf16[384,4096]{1,0:T(8,128)(2,1)} %convolution_convert_fusion), channel_id=1, source_target_pairs={{0,8},{1,9},{2,10},{3,11},{4,12},{5,13},{6,14},{7,15},{8,0},{9,1},... | collective-permute-start | bytes 9437192 | tf_op jit(solution)/shard_map/ppermute | solution.py:30
  140.0 19.4 %collective-permute-start.12 = (bf16[384,1024]{1,0:T(8,128)(2,1)}, bf16[384,1024]{1,0:T(8,128)(2,1)}, u32[]{:S(2)}, u32[]{:S(2)}) collective-permute-start(bf16[384,1024]{1,0:T(8,128)(2,1)} %multiply_convert_fusion), channel_id=1, source_target_pairs={{0,1},{1,0},{2,3},{3,2},{4,5},{5,4},{6,7},{7,6},{8,9},{9,8},{10,11... | collective-permute-start | bytes 2359304 | tf_op jit(solution)/shard_map/ppermute | solution.py:30
  140.2 20.3 %collective-permute-start.13 = (bf16[384,1024]{1,0:T(8,128)(2,1)}, bf16[384,1024]{1,0:T(8,128)(2,1)}, u32[]{:S(2)}, u32[]{:S(2)}) collective-permute-start(bf16[384,1024]{1,0:T(8,128)(2,1)} %multiply_convert_fusion), channel_id=1, source_target_pairs={{0,3},{1,2},{2,1},{3,0},{4,7},{5,6},{6,5},{7,4},{8,11},{9,10},{10,... | collective-permute-start | bytes 2359304 | tf_op jit(solution)/shard_map/ppermute | solution.py:30
  143.5 30.2 %collective-permute-start.11 = (bf16[384,1024]{1,0:T(8,128)(2,1)}, bf16[384,1024]{1,0:T(8,128)(2,1)}, u32[]{:S(2)}, u32[]{:S(2)}) collective-permute-start(bf16[384,1024]{1,0:T(8,128)(2,1)} %bitcast.15), channel_id=1, source_target_pairs={{0,4},{1,5},{2,6},{3,7},{4,0},{5,1},{6,2},{7,3},{8,12},{9,13},{10,... | collective-permute-start | bytes 2359304 | tf_op jit(solution)/shard_map/ppermute | solution.py:30
  162.9 61.0 %collective-permute-start.17 = (bf16[1536,1024]{1,0:T(8,128)(2,1)S(1)}, bf16[1536,1024]{1,0:T(8,128)(2,1)}, u32[]{:S(2)}, u32[]{:S(2)}) collective-permute-start(bf16[1536,1024]{1,0:T(8,128)(2,1)S(1)} %bitcast.90), channel_id=1, source_target_pairs={{0,8},{1,9},{2,10},{3,11},{4,12},{5,13},{6,14},{7,15},{8,0},{9,1},... | collective-permute-start | bytes 9437192 | tf_op jit(solution)/shard_map/ppermute | solution.py:30
  171.7 57.4 %collective-permute-start.19 = (bf16[384,1024]{1,0:T(8,128)(2,1)}, bf16[384,1024]{1,0:T(8,128)(2,1)}, u32[]{:S(2)}, u32[]{:S(2)}) collective-permute-start(bf16[384,1024]{1,0:T(8,128)(2,1)} %collective-permute-done.12), channel_id=1, source_target_pairs={{0,3},{1,2},{2,1},{3,0},{4,7},{5,6},{6,5},{7,4},{8,11},{9,10},{10,... | collective-permute-start | bytes 2359304 | tf_op jit(solution)/shard_map/ppermute | solution.py:30
  177.0 29.0 %all-to-all-start.2 = ((bf16[16,24,1024]{2,1,0:T(8,128)(2,1)}), bf16[16,24,1024]{2,1,0:T(8,128)(2,1)}, u32[]{:S(2)}, u32[]{:S(2)}) async-start(bf16[16,24,1024]{2,1,0:T(8,128)(2,1)} %bitcast.99), calls=%async_computation.2 | async-start | bytes 1572864 | tf_op jit(solution)/shard_map/all_to_all | solution.py:178
  191.4 30.1 %collective-permute-start.18 = (bf16[384,1024]{1,0:T(8,128)(2,1)}, bf16[384,1024]{1,0:T(8,128)(2,1)}, u32[]{:S(2)}, u32[]{:S(2)}) collective-permute-start(bf16[384,1024]{1,0:T(8,128)(2,1)} %copy-done.14), channel_id=1, source_target_pairs={{0,1},{1,0},{2,3},{3,2},{4,5},{5,4},{6,7},{7,6},{8,9},{9,8},{10,11... | collective-permute-start | bytes 2359304 | tf_op jit(solution)/shard_map/ppermute | solution.py:30
  206.0 63.4 %all-to-all-start.3 = ((bf16[16,24,4096]{2,1,0:T(8,128)(2,1)}), bf16[16,24,4096]{2,1,0:T(8,128)(2,1)}, u32[]{:S(2)}, u32[]{:S(2)}) async-start(bf16[16,24,4096]{2,1,0:T(8,128)(2,1)} %bitcast.98), calls=%async_computation.3 | async-start | bytes 6291456 | tf_op jit(solution)/shard_map/all_to_all | solution.py:65
  232.4 43.8 %collective-permute-start.20 = (bf16[512,1024]{1,0:T(8,128)(2,1)S(1)}, bf16[512,1024]{1,0:T(8,128)(2,1)S(1)}, u32[]{:S(2)}, u32[]{:S(2)}) collective-permute-start(bf16[512,1024]{1,0:T(8,128)(2,1)S(1)} %get-tuple-element.44), channel_id=1, source_target_pairs={{0,4},{1,5},{2,6},{3,7},{4,0},{5,1},{6,2},{7,3},{8,12},{9,13},{10,... | collective-permute-start | bytes 3145736 | tf_op jit(solution)/shard_map/ppermute | solution.py:30
  (21 other events, 190.0 us)
Sparse Core Ops, SparseCore 0:
  168.9 47.7 reduce-scatter.1
where the time goes:
time: 295 us; the launch traced here: 292 us
  waiting for transfers between devices  89.8 us (30%)
  starting transfers between devices  77.2 us (26%)
  matrix products  64.6 us (22%)
  local copies, waits for them, and re-layouts  35.3 us (12%)
  between operations  14.5 us (5%)
  other arithmetic  9.79 us (3%)
    dot_general x13, matrix products, dot(): return lax.dot_general(a, b, (dims, ((), ())), preferred_element_type=F32)  59.5 us
    ppermute x15, waiting for transfers between devices, swap(): return lax.ppermute(v, AXES, pairs)  44 us
    all_to_all x2, waiting for transfers between devices, exchange(): return lax.all_to_all(v, AXES, 0, 0, axis_index_groups=members, tiled=True)  30.9 us
    ppermute x15, starting transfers between devices, swap(): return lax.ppermute(v, AXES, pairs)  20.4 us
    all_to_all x1, starting transfers between devices, on_device(): outs = lax.all_to_all(output, 'expert', 0, 0, tiled=True)  14.4 us
    all_to_all x2, starting transfers between devices, exchange(): return lax.all_to_all(v, AXES, 0, 0, axis_index_groups=members, tiled=True)  11.5 us
    ppermute x6, waiting for transfers between devices, swap_split(): return lax.ppermute(v, AXES, pairs)  10.6 us
    all_to_all x1, starting transfers between devices, on_device(): lax.all_to_all(gates[0].reshape(8, 16, 24).transpose(1, 0, 2), 'expert',...  8.84 us
  transfers between devices with their start and end apart: 28, of which 13 were waited for; matrix products, arithmetic and copies ran while one was open for 36% of the time, Pallas kernels for 0%

commit v1 on v0

--- a/solution.py
+++ b/solution.py
@@ -58,6 +58,7 @@
 
 
 PLANE = groups(lambda x, y, zh, zl, c: (y, c), lambda x, y, zh, zl, c: (x, zl, zh))
+LEVEL = groups(lambda x, y, zh, zl, c: y, lambda x, y, zh, zl, c: (c, x, zl, zh))
 RING = groups(lambda x, y, zh, zl, c: (x, zh, zl, c), lambda x, y, zh, zl, c: y)
 
 
@@ -79,10 +80,17 @@
         out[at[i]] = refs[i // 4][i % 4]
 
 
-def place(at, lines):
+def place_columns_kernel(at, *refs):
+    out = refs[4]
+    for i in range(16):
+        for k in range(4):
+            out[k, at[i]] = refs[i // 4][i % 4, k]
+
+
+def place(kernel, shape, at, lines):
     return pl.pallas_call(
-        place_kernel,
-        out_shape=jax.ShapeDtypeStruct((16,) + lines[0].shape[1:], lines[0].dtype),
+        kernel,
+        out_shape=jax.ShapeDtypeStruct(shape, lines[0].dtype),
         in_specs=[pl.BlockSpec(memory_space=pltpu.SMEM)]
         + [pl.BlockSpec(memory_space=pltpu.VMEM)] * 4,
         out_specs=pl.BlockSpec(memory_space=pltpu.VMEM),
@@ -91,10 +99,6 @@
     )(at, *lines)
 
 
-def gather(v, members):
-    return exchange(jnp.broadcast_to(v[None], (len(members[0]),) + v.shape), members)
-
-
 def on_device(trunk, w_first, w_second, gates, d_mixed):
     e = lax.axis_index("expert")
     d = lax.axis_index("dp")
@@ -111,13 +115,19 @@
     dx, dz = x ^ (jnp.arange(16) // 4), zz ^ (jnp.arange(16) % 4)
     ex, ez = x ^ (jnp.arange(16) % 4), zz ^ (jnp.arange(16) // 4)
     at = jnp.where(c == 0, dx * 4 + dz, ex * 4 + ez).astype(jnp.int32)
-    own = place(at, [line, far[1], far[0], far[2]]).reshape(384, 4096)
-
+    own = place(place_kernel, (16, 24, 4096), at, [line, far[1], far[0], far[2]])
+    own = own.reshape(384, 4096)
+
+    gate_order = after(gate_rows, line).reshape(2, 4, 2, 8, 24)
+    gate_order = gate_order.transpose(2, 1, 0, 3, 4).reshape(16, 8, 24)
     d_out_each = jnp.einsum(
-        "etr,rto->ero", gate_rows, d_mixed, preferred_element_type=F32
+        "etr,rto->ero", gate_order, d_mixed, preferred_element_type=F32
     ).astype(BF)
-    back = lax.all_to_all(d_out_each, "expert", 0, 0, tiled=True)
-
+    d_out_each = d_out_each.reshape(8, 1, 2, 24, 1024)
+    d_out_each = jnp.broadcast_to(d_out_each, (8, 2, 2, 24, 1024)).reshape(32, 24, 1024)
+    back = exchange(d_out_each, LEVEL)
+
+    trunk, w_first, _ = lax.optimization_barrier((trunk, w_first, d_out_each))
     half = lax.dynamic_slice_in_dim(w_first[0], zl * 1024, 1024, 1)
     cols = trunk.reshape(24, 2, 4, 512)
     t_y = [pick(cols, y ^ k, 2).reshape(24, 1024) for k in range(4)]
@@ -125,9 +135,9 @@
 
     own, back, half, t_y = lax.optimization_barrier((own, back, half, t_y))
     other = swap(own, c=1)
-    back = back.reshape(2, 4, 2, 24, 1024)
-    back_z = swap(back, z=1)
-    wide = gather(t_y, PLANE).reshape(16, 4, 24, 1024)
+    wide = jnp.stack([t_y] + [swap_split(t_y, k, True) for k in (1, 2, 3)])
+    back = back.reshape(2, 384, 1024)
+    d_output = jnp.where(c == 0, back, back[::-1]).reshape(768, 1024)
     second = w_second[0]
     second_own = lax.dynamic_slice_in_dim(second, zl * 1024, 1024, 0)
     second_far = lax.dynamic_slice_in_dim(second, (1 - zl) * 1024, 1024, 0)
@@ -143,39 +153,46 @@
         return (d_hidden * slope).astype(BF)
 
     hidden_own, slope_own = forward(own)
-    hidden_own, back_z, other = lax.optimization_barrier((hidden_own, back_z, other))
-    pair = jnp.where(zl == 0, jnp.stack([back, back_z]), jnp.stack([back_z, back]))
-    pair = pair.transpose(3, 2, 0, 1, 4, 5)
-    d_output = jnp.where(c == 0, pair, pair[::-1]).reshape(768, 1024)
-
     d_own = backward(d_output[:384], slope_own)
+    d_own, other, wide = lax.optimization_barrier((d_own, other, wide))
     near_own = (swap(d_own, y=1), swap(d_own, y=3))
     hidden_other, slope_other = forward(other)
     d_other = backward(d_output[384:], slope_other)
     near_other = (swap(d_other, y=1), swap(d_other, y=3))
 
-    d_other_late, *near_own = lax.optimization_barrier((d_other, *near_own))
-    dt_other = dot(d_other_late, half, ((1,), (1,))).astype(BF)
-    far_own = swap(near_own[1], y=1)
     hidden = jnp.concatenate([hidden_own, hidden_other])
-    d_own_late, *near_other = lax.optimization_barrier((d_own, *near_other))
-    dt = dot(d_own_late, half, ((1,), (1,))) + swap(dt_other, c=1).astype(F32)
-    dt = dt.astype(BF)
-    far_other = swap(near_other[0], y=3)
-
-    ds = dot(hidden, d_output, ((0,), (0,))).astype(BF)
-    d_second = lax.psum_scatter(
-        ds, AXES, axis_index_groups=RING, scatter_dimension=0, tiled=True
-    )
-
     by_z = hidden.reshape(8, 2, 48, 1024)
     mine = pick(by_z, zl, 1).reshape(384, 1024)
     theirs = swap(pick(by_z, 1 - zl, 1).reshape(384, 1024), z=1)
+    mine, near_own = lax.optimization_barrier((mine, near_own))
     output = dot(mine, second_own, ((1,), (0,))) + dot(theirs, second_far, ((1,), (0,)))
     output = output.astype(BF).reshape(2, 4, 2, 24, 1024)
     output = jnp.where(c == 0, output, output[::-1])
     output = output.transpose(2, 1, 0, 3, 4).reshape(16, 24, 1024)
+
+    d_other_late, output = lax.optimization_barrier((d_other, output))
     outs = lax.all_to_all(output, "expert", 0, 0, tiled=True)
+    far_own = swap(near_own[1], y=1)
+    wide_far = [swap_split(wide, k, False) for k in (2, 1, 3)]
+    dt_other = dot(d_other_late, half, ((1,), (1,))).astype(BF)
+    d_own_late, near_other, wide_far, hidden, outs = lax.optimization_barrier(
+        (d_own, near_other, wide_far, hidden, outs)
+    )
+    far_other = swap(near_other[0], y=3)
+    dt = dot(d_own_late, half, ((1,), (1,))) + swap(dt_other, c=1).astype(F32)
+    dt = exchange(dt.astype(BF).reshape(16, 24, 4096), PLANE)
+    d_trunk = jnp.sum(dt, axis=0, dtype=F32).astype(BF)
+    wide = place(
+        place_columns_kernel, (4, 16, 24, 1024), at,
+        [wide, wide_far[1], wide_far[0], wide_far[2]],
+    ).reshape(1536, 1024)
+    wide_other = swap(wide, c=1)
+
+    ds = dot(hidden, d_output, ((0,), (0,))).astype(BF)
+    d_second = lax.psum_scatter(
+        ds, AXES, axis_index_groups=RING, scatter_dimension=0, tiled=True
+    )
+
     mixed = jnp.einsum(
         "etr,ero->rto", gate_rows, outs, preferred_element_type=F32
     ).astype(BF)
@@ -183,14 +200,10 @@
         "rto,ero->etr", d_mixed, outs, preferred_element_type=F32
     ).astype(BF)
 
-    dt = exchange(after(dt, outs).reshape(16, 24, 4096), PLANE)
-    d_trunk = jnp.sum(dt, axis=0, dtype=F32).astype(BF)
     d_gate = lax.all_to_all(after(d_gate, dt), "expert", 0, 0, tiled=True)
     d_gate = d_gate.transpose(1, 0, 2).reshape(8, 384)
 
-    wide = after(wide, *near_other)
-    wide = wide.transpose(1, 0, 2, 3).reshape(1536, 1024)
-    wide_other = swap(wide, c=1)
+    wide, far_own = lax.optimization_barrier((wide, far_own))
     tile = dot(wide[:1152], jnp.concatenate([d_own, *near_own]), ((0,), (0,)))
     tile = tile + dot(wide_other[:1152], jnp.concatenate([d_other, *near_other]), ((0,), (0,)))
     tile = tile + dot(wide[1152:], far_own, ((0,), (0,)))

time: 295 us -> 322 us (1.092)
  the two profiles are of different devices: /device:TPU:1 before, /device:TPU:38 now
where the time goes in v1:
time: 322 us; the launch traced here: 317 us
  waiting for transfers between devices  108 us (34%)
  starting transfers between devices  79.7 us (25%)
  matrix products  64.8 us (20%)
  local copies, waits for them, and re-layouts  36.6 us (11%)
  between operations  14.7 us (5%)
  other arithmetic  11 us (3%)
    ppermute x14, waiting for transfers between devices, swap(): return lax.ppermute(v, AXES, pairs)  60.6 us
    dot_general x13, matrix products, dot(): return lax.dot_general(a, b, (dims, ((), ())), preferred_element_type=F32)  59.7 us
    ppermute x14, starting transfers between devices, swap(): return lax.ppermute(v, AXES, pairs)  24.4 us
    all_to_all x2, waiting for transfers between devices, exchange(): return lax.all_to_all(v, AXES, 0, 0, axis_index_groups=members, tiled=True)  23 us
    ppermute x12, waiting for transfers between devices, swap_split(): return lax.ppermute(v, AXES, pairs)  19.6 us
    ppermute x12, starting transfers between devices, swap_split(): return lax.ppermute(v, AXES, pairs)  17.6 us
    all_to_all x2, starting transfers between devices, exchange(): return lax.all_to_all(v, AXES, 0, 0, axis_index_groups=members, tiled=True)  17.4 us
    unnamed x45, local copies, waits for them, and re-layouts  12.5 us
  transfers between devices with their start and end apart: 32, of which 12 were waited for; matrix products, arithmetic and copies ran while one was open for 28% of the time, Pallas kernels for 0%

profile of v1, /device:TPU:38, one launch (start us, length us, event | category | flops | bytes accessed | tf_op | source)
XLA Modules:
  0.0 316.7 jit_solution(3280783975342226057)
XLA Ops:
  12.8 7.8 %all-to-all-start = ((bf16[16,8,24]{2,1,0:T(8,128)(2,1)}), bf16[16,8,24]{2,1,0:T(8,128)(2,1)S(1)}, u32[]{:S(2)}, u32[]{:S(2)}) async-start(bf16[16,8,24]{2,1,0:T(8,128)(2,1)} %copy.28), calls=%async_computation | async-start | bytes 65536 | tf_op jit(solution)/shard_map/all_to_all | solution.py:109
  21.6 4.6 %all-to-all-done = bf16[16,8,24]{2,1,0:T(8,128)(2,1)S(1)} async-done(((bf16[16,8,24]{2,1,0:T(8,128)(2,1)}), bf16[16,8,24]{2,1,0:T(8,128)(2,1)S(1)}, u32[]{:S(2)}, u32[]{:S(2)}) %all-to-all-start) | async-done | bytes 6176 | tf_op jit(solution)/shard_map/all_to_all | solution.py:109
  28.6 5.9 %all-to-all-start.1 = ((bf16[32,24,1024]{2,1,0:T(8,128)(2,1)}), bf16[32,24,1024]{2,1,0:T(8,128)(2,1)}, u32[]{:S(2)}, u32[]{:S(2)}) async-start(bf16[32,24,1024]{2,1,0:T(8,128)(2,1)} %bitcast.11), calls=%async_computation.1 | async-start | bytes 3145728 | tf_op jit(solution)/shard_map/all_to_all | solution.py:66
  41.1 3.2 %dynamic-slice_reduce_fusion.3 = (bf16[24,2,512]{2,1,0:T(2,128)(2,1)}, bf16[24,2,512]{2,1,0:T(2,128)(2,1)}, bf16[24,2,512]{2,1,0:T(2,128)(2,1)}, bf16[24,2,512]{2,1,0:T(2,128)(2,1)S(1)}) fusion(bf16[24,2,4,512]{3,2,1,0:T(4,128)(2,1)} %reshape.132, s32[]{:T(128)S(6)} %select_n.124, s32[]{:T(128)S(6)} %select_n.126, s32[]{:T(128)S(6)} %select_n.125, ...), kind=kLoop, calls=%fused_computation.64 | loop fusion | bytes 393232 | tf_op jit(solution)/shard_map/jit(dynamic_index_in_dim)/dynamic_slice | solution.py:74
  44.9 3.2 %collective-permute-start.8 = (bf16[24,1024]{1,0:T(8,128)(2,1)}, bf16[24,1024]{1,0:T(8,128)(2,1)}, u32[]{:S(2)}, u32[]{:S(2)}) collective-permute-start(bf16[24,1024]{1,0:T(8,128)(2,1)} %bitcast.47), channel_id=1, source_target_pairs={{0,2},{1,3},{2,0},{3,1},{4,6},{5,7},{6,4},{7,5},{8,10},{9,11},{10,... | collective-permute-start | bytes 147464 | tf_op jit(solution)/shard_map/ppermute | solution.py:30
  52.5 7.6 %dynamic-slice_bitcast_fusion = bf16[4096,1024]{1,0:T(8,128)(2,1)} fusion(bf16[1,4096,2048]{2,1,0:T(8,128)(2,1)} %param.6, s32[]{:T(128)S(6)} %select_n.122), kind=kLoop, calls=%fused_computation | loop fusion | bytes 16777220 | tf_op jit(solution)/shard_map/dynamic_slice | solution.py:131
  63.4 9.0 %collective-permute-done.4.refs_2_ = bf16[4,24,4096]{2,1,0:T(8,128)(2,1)S(1)} collective-permute-done((bf16[4,24,4096]{2,1,0:T(8,128)(2,1)S(1)}, bf16[4,24,4096]{2,1,0:T(8,128)(2,1)S(1)}, u32[]{:S(2)}, u32[]{:S(2)}) %collective-permute-start.4) | collective-permute-done | bytes 786464 | tf_op jit(solution)/shard_map/ppermute | solution.py:42
  81.2 6.6 %multiply_convert_fusion.1 = (bf16[384,1024]{1,0:T(8,128)(2,1)S(1)}, f32[384,1024]{1,0:T(8,128)S(1)}) fusion(bf16[384,4096]{1,0:T(8,128)(2,1)S(1)} %bitcast.94, bf16[4096,1024]{1,0:T(8,128)(2,1)} %dynamic-slice_bitcast_fusion), kind=kOutput, calls=%fused_computation.36 | convolution fusion | flops 3223191552 | bytes 13893632 | tf_op jit(solution)/shard_map/dot_general | solution.py:70
  94.2 6.5 %multiply_convert_fusion = (bf16[384,1024]{1,0:T(8,128)(2,1)S(1)}, f32[384,1024]{1,0:T(8,128)}) fusion(bf16[384,4096]{1,0:T(8,128)(2,1)} %collective-permute-done.9, bf16[4096,1024]{1,0:T(8,128)(2,1)S(1)} %bitcast.96), kind=kOutput, calls=%fused_computation.35 | convolution fusion | flops 3223191552 | bytes 13893632 | tf_op jit(solution)/shard_map/dot_general | solution.py:70
  103.2 4.5 %multiply_convert_fusion.2 = bf16[384,1024]{1,0:T(8,128)(2,1)} fusion(f32[384,1024]{1,0:T(8,128)} %get-tuple-element.66, bf16[1,2048,1024]{2,1,0:T(8,128)(2,1)} %param.7, s32[]{:T(128)S(6)} %select_n.122, bf16[2,384,1024]{2,1,0:T(8,128)(2,1)} %copy-done.13), kind=kOutput, calls=%fused_computation.37 | convolution fusion | flops 808845312 | bytes 5242884 | tf_op jit(solution)/shard_map/dot_general | solution.py:70
  112.9 8.6 %collective-permute-done.20 = bf16[384,1024]{1,0:T(8,128)(2,1)} collective-permute-done((bf16[384,1024]{1,0:T(8,128)(2,1)}, bf16[384,1024]{1,0:T(8,128)(2,1)}, u32[]{:S(2)}, u32[]{:S(2)}) %collective-permute-start.20) | collective-permute-done | bytes 786464 | tf_op jit(solution)/shard_map/ppermute | solution.py:30
  125.8 8.8 %convolution_convert_fusion = bf16[384,4096]{1,0:T(8,128)(2,1)} fusion(bf16[384,1024]{1,0:T(8,128)(2,1)} %multiply_convert_fusion.2, bf16[4096,1024]{1,0:T(8,128)(2,1)} %dynamic-slice_bitcast_fusion), kind=kOutput, calls=%fused_computation.2 | convolution fusion | flops 3222798336 | bytes 12320768 | tf_op jit(solution)/shard_map/dot_general | solution.py:70
  139.1 15.7 %collective-permute-done.13 = bf16[384,1024]{1,0:T(8,128)(2,1)} collective-permute-done((bf16[384,1024]{1,0:T(8,128)(2,1)}, bf16[384,1024]{1,0:T(8,128)(2,1)}, u32[]{:S(2)}, u32[]{:S(2)}) %collective-permute-start.13) | collective-permute-done | bytes 786464 | tf_op jit(solution)/shard_map/ppermute | solution.py:30
  157.0 5.2 %all-to-all-start.2 = ((bf16[16,24,1024]{2,1,0:T(8,128)(2,1)}), bf16[16,24,1024]{2,1,0:T(8,128)(2,1)}, u32[]{:S(2)}, u32[]{:S(2)}) async-start(bf16[16,24,1024]{2,1,0:T(8,128)(2,1)} %bitcast.100), calls=%async_computation.2 | async-start | bytes 1572864 | tf_op jit(solution)/shard_map/all_to_all | solution.py:174
  164.0 10.4 %collective-permute-done.17.refs_3_ = bf16[4,4,24,1024]{3,2,1,0:T(8,128)(2,1)S(1)} collective-permute-done((bf16[4,4,24,1024]{3,2,1,0:T(8,128)(2,1)S(1)}, bf16[4,4,24,1024]{3,2,1,0:T(8,128)(2,1)S(1)}, u32[]{:S(2)}, u32[]{:S(2)}) %collective-permute-start.17) | collective-permute-done | bytes 786464 | tf_op jit(solution)/shard_map/ppermute | solution.py:42
  181.3 10.7 %collective-permute-start.23 = (bf16[1536,1024]{1,0:T(8,128)(2,1)S(1)}, bf16[1536,1024]{1,0:T(8,128)(2,1)}, u32[]{:S(2)}, u32[]{:S(2)}) collective-permute-start(bf16[1536,1024]{1,0:T(8,128)(2,1)S(1)} %bitcast.90), channel_id=1, source_target_pairs={{0,8},{1,9},{2,10},{3,11},{4,12},{5,13},{6,14},{7,15},{8,0},{9,1},... | collective-permute-start | bytes 9437192 | tf_op jit(solution)/shard_map/ppermute | solution.py:30
  196.7 19.5 %collective-permute-done.22 = bf16[384,1024]{1,0:T(8,128)(2,1)} collective-permute-done((bf16[384,1024]{1,0:T(8,128)(2,1)}, bf16[384,1024]{1,0:T(8,128)(2,1)}, u32[]{:S(2)}, u32[]{:S(2)}) %collective-permute-start.22) | collective-permute-done | bytes 786464 | tf_op jit(solution)/shard_map/ppermute | solution.py:30
  216.3 9.7 %add_convert_fusion = bf16[384,4096]{1,0:T(8,128)(2,1)} fusion(bf16[384,4096]{1,0:T(8,128)(2,1)} %collective-permute-done.21, bf16[384,1024]{1,0:T(8,128)(2,1)} %multiply_convert_fusion.3, bf16[4096,1024]{1,0:T(8,128)(2,1)} %dynamic-slice_bitcast_fusion), kind=kOutput, calls=%fused_computation.1 | convolution fusion | flops 3225944064 | bytes 15466496 | tf_op jit(solution)/shard_map/dot_general | solution.py:70
  226.0 11.5 %all-to-all-start.3 = ((bf16[16,24,4096]{2,1,0:T(8,128)(2,1)}), bf16[16,24,4096]{2,1,0:T(8,128)(2,1)}, u32[]{:S(2)}, u32[]{:S(2)}) async-start(bf16[16,24,4096]{2,1,0:T(8,128)(2,1)} %bitcast.99), calls=%async_computation.3 | async-start | bytes 6291456 | tf_op jit(solution)/shard_map/all_to_all | solution.py:66
  237.5 4.4 %fusion.2 = f32[1024,1024]{1,0:T(8,128)S(1)} fusion(bf16[384,1024]{1,0:T(8,128)(2,1)} %collective-permute-done.19, bf16[384,1024]{1,0:T(8,128)(2,1)} %collective-permute-done.18, bf16[384,1024]{1,0:T(8,128)(2,1)} %multiply_convert_fusion.3, bf16[1536,1024]{1,0:T(8,128)(2,1)S(1)} %bitcast.91), kind=kOutput, calls=%fused_computation.7 | convolution fusion | flops 2422996992 | bytes 8912896 | tf_op jit(solution)/shard_map/dot_general | solution.py:70
  244.3 5.2 %fusion = f32[1024,1024]{1,0:T(8,128)S(1)} fusion(bf16[1536,1024]{1,0:T(8,128)(2,1)} %collective-permute-done.23, bf16[384,1024]{1,0:T(8,128)(2,1)} %collective-permute-done.14, bf16[384,1024]{1,0:T(8,128)(2,1)} %collective-permute-done.13, bf16[384,1024]{1,0:T(8,128)(2,1)} %multiply_convert_fusion.2), kind=kOutput, calls=%fused_computation.5 | convolution fusion | flops 2422996992 | bytes 8912896 | tf_op jit(solution)/shard_map/dot_general | solution.py:70
  259.6 23.0 %all-to-all-done.3 = bf16[16,24,4096]{2,1,0:T(8,128)(2,1)} async-done(((bf16[16,24,4096]{2,1,0:T(8,128)(2,1)}), bf16[16,24,4096]{2,1,0:T(8,128)(2,1)}, u32[]{:S(2)}, u32[]{:S(2)}) %all-to-all-start.3) | async-done | bytes 3145760 | tf_op jit(solution)/shard_map/all_to_all | solution.py:66
  284.1 7.3 %all-to-all-start.4 = ((bf16[16,8,24]{2,1,0:T(8,128)(2,1)}), bf16[16,8,24]{2,1,0:T(8,128)(2,1)}, u32[]{:S(2)}, u32[]{:S(2)}) async-start(bf16[16,8,24]{2,1,0:T(8,128)(2,1)} %copy.40), calls=%async_computation.4 | async-start | bytes 65536 | tf_op jit(solution)/shard_map/all_to_all | solution.py:203
  291.5 11.5 %collective-permute-done.25 = bf16[512,1024]{1,0:T(8,128)(2,1)S(1)} collective-permute-done((bf16[512,1024]{1,0:T(8,128)(2,1)S(1)}, bf16[512,1024]{1,0:T(8,128)(2,1)S(1)}, u32[]{:S(2)}, u32[]{:S(2)}) %collective-permute-start.25) | collective-permute-done | bytes 1048608 | tf_op jit(solution)/shard_map/ppermute | solution.py:30
  (131 shorter events, 91.5 us)
Async XLA Ops:
  28.6 46.2 %all-to-all-start.1 = ((bf16[32,24,1024]{2,1,0:T(8,128)(2,1)}), bf16[32,24,1024]{2,1,0:T(8,128)(2,1)}, u32[]{:S(2)}, u32[]{:S(2)}) async-start(bf16[32,24,1024]{2,1,0:T(8,128)(2,1)} %bitcast.11), calls=%async_computation.1 | async-start | bytes 3145728 | tf_op jit(solution)/shard_map/all_to_all | solution.py:66
  34.6 28.8 %collective-permute-start.3 = (bf16[4,24,4096]{2,1,0:T(8,128)(2,1)S(1)}, bf16[4,24,4096]{2,1,0:T(8,128)(2,1)S(1)}, u32[]{:S(2)}, u32[]{:S(2)}) collective-permute-start(bf16[4,24,4096]{2,1,0:T(8,128)(2,1)S(1)} %pad_maximum_fusion.1.refs_0_), channel_id=1, source_target_pairs={{0,16},{1,17},{2,18},{3,19},{4,20},{5,21},{6,22},{7,23},{8,72},{9,... | collective-permute-start | bytes 2359304 | tf_op jit(solution)/shard_map/ppermute | solution.py:42
  35.5 36.9 %collective-permute-start.4 = (bf16[4,24,4096]{2,1,0:T(8,128)(2,1)S(1)}, bf16[4,24,4096]{2,1,0:T(8,128)(2,1)S(1)}, u32[]{:S(2)}, u32[]{:S(2)}) collective-permute-start(bf16[4,24,4096]{2,1,0:T(8,128)(2,1)S(1)} %pad_maximum_fusion.1.refs_0_), channel_id=1, source_target_pairs={{0,32},{1,33},{2,34},{3,35},{4,36},{5,37},{6,38},{7,39},{8,12},{9,... | collective-permute-start | bytes 2359304 | tf_op jit(solution)/shard_map/ppermute | solution.py:42
  36.8 35.6 %collective-permute-start.5 = (bf16[4,24,4096]{2,1,0:T(8,128)(2,1)S(1)}, bf16[4,24,4096]{2,1,0:T(8,128)(2,1)S(1)}, u32[]{:S(2)}, u32[]{:S(2)}) collective-permute-start(bf16[4,24,4096]{2,1,0:T(8,128)(2,1)S(1)} %pad_maximum_fusion.1.refs_0_), channel_id=1, source_target_pairs={{0,48},{1,49},{2,50},{3,51},{4,52},{5,53},{6,54},{7,55},{8,76},{9,... | collective-permute-start | bytes 2359304 | tf_op jit(solution)/shard_map/ppermute | solution.py:42
  74.8 15.3 %collective-permute-start.9 = (bf16[384,4096]{1,0:T(8,128)(2,1)}, bf16[384,4096]{1,0:T(8,128)(2,1)}, u32[]{:S(2)}, u32[]{:S(2)}) collective-permute-start(bf16[384,4096]{1,0:T(8,128)(2,1)} %bitcast.93), channel_id=1, source_target_pairs={{0,8},{1,9},{2,10},{3,11},{4,12},{5,13},{6,14},{7,15},{8,0},{9,1},... | collective-permute-start | bytes 9437192 | tf_op jit(solution)/shard_map/ppermute | solution.py:30
  74.9 15.1 %collective-permute-start.12 = (bf16[4,24,1024]{2,1,0:T(8,128)(2,1)}, bf16[4,24,1024]{2,1,0:T(8,128)(2,1)S(1)}, u32[]{:S(2)}, u32[]{:S(2)}) collective-permute-start(bf16[4,24,1024]{2,1,0:T(8,128)(2,1)} %pad_maximum_fusion.3), channel_id=1, source_target_pairs={{0,68},{1,69},{2,70},{3,71},{4,64},{5,65},{6,66},{7,67},{8,56},{9,... | collective-permute-start | bytes 589832 | tf_op jit(solution)/shard_map/ppermute | solution.py:42
  75.7 14.3 %collective-permute-start.11 = (bf16[4,24,1024]{2,1,0:T(8,128)(2,1)}, bf16[4,24,1024]{2,1,0:T(8,128)(2,1)S(1)}, u32[]{:S(2)}, u32[]{:S(2)}) collective-permute-start(bf16[4,24,1024]{2,1,0:T(8,128)(2,1)} %pad_maximum_fusion.3), channel_id=1, source_target_pairs={{0,4},{1,5},{2,6},{3,7},{4,0},{5,1},{6,2},{7,3},{8,40},{9,41},{10,... | collective-permute-start | bytes 589832 | tf_op jit(solution)/shard_map/ppermute | solution.py:42
  90.1 20.3 %collective-permute-start.18 = (bf16[384,1024]{1,0:T(8,128)(2,1)}, bf16[384,1024]{1,0:T(8,128)(2,1)}, u32[]{:S(2)}, u32[]{:S(2)}) collective-permute-start(bf16[384,1024]{1,0:T(8,128)(2,1)} %multiply_convert_fusion.3), channel_id=1, source_target_pairs={{0,1},{1,0},{2,3},{3,2},{4,5},{5,4},{6,7},{7,6},{8,9},{9,8},{10,11... | collective-permute-start | bytes 2359304 | tf_op jit(solution)/shard_map/ppermute | solution.py:30
  92.1 20.9 %collective-permute-start.19 = (bf16[384,1024]{1,0:T(8,128)(2,1)}, bf16[384,1024]{1,0:T(8,128)(2,1)}, u32[]{:S(2)}, u32[]{:S(2)}) collective-permute-start(bf16[384,1024]{1,0:T(8,128)(2,1)} %multiply_convert_fusion.3), channel_id=1, source_target_pairs={{0,3},{1,2},{2,1},{3,0},{4,7},{5,6},{6,5},{7,4},{8,11},{9,10},{10,... | collective-permute-start | bytes 2359304 | tf_op jit(solution)/shard_map/ppermute | solution.py:30
  102.1 19.4 %collective-permute-start.20 = (bf16[384,1024]{1,0:T(8,128)(2,1)}, bf16[384,1024]{1,0:T(8,128)(2,1)}, u32[]{:S(2)}, u32[]{:S(2)}) collective-permute-start(bf16[384,1024]{1,0:T(8,128)(2,1)} %bitcast.26), channel_id=1, source_target_pairs={{0,4},{1,5},{2,6},{3,7},{4,0},{5,1},{6,2},{7,3},{8,12},{9,13},{10,... | collective-permute-start | bytes 2359304 | tf_op jit(solution)/shard_map/ppermute | solution.py:30
  134.6 81.6 %collective-permute-start.21 = (bf16[384,4096]{1,0:T(8,128)(2,1)}, bf16[384,4096]{1,0:T(8,128)(2,1)}, u32[]{:S(2)}, u32[]{:S(2)}) collective-permute-start(bf16[384,4096]{1,0:T(8,128)(2,1)} %convolution_convert_fusion), channel_id=1, source_target_pairs={{0,8},{1,9},{2,10},{3,11},{4,12},{5,13},{6,14},{7,15},{8,0},{9,1},... | collective-permute-start | bytes 9437192 | tf_op jit(solution)/shard_map/ppermute | solution.py:30
  134.6 20.3 %collective-permute-start.13 = (bf16[384,1024]{1,0:T(8,128)(2,1)}, bf16[384,1024]{1,0:T(8,128)(2,1)}, u32[]{:S(2)}, u32[]{:S(2)}) collective-permute-start(bf16[384,1024]{1,0:T(8,128)(2,1)} %multiply_convert_fusion.2), channel_id=1, source_target_pairs={{0,1},{1,0},{2,3},{3,2},{4,5},{5,4},{6,7},{7,6},{8,9},{9,8},{10,11... | collective-permute-start | bytes 2359304 | tf_op jit(solution)/shard_map/ppermute | solution.py:30
  135.3 26.9 %collective-permute-start.14 = (bf16[384,1024]{1,0:T(8,128)(2,1)}, bf16[384,1024]{1,0:T(8,128)(2,1)}, u32[]{:S(2)}, u32[]{:S(2)}) collective-permute-start(bf16[384,1024]{1,0:T(8,128)(2,1)} %multiply_convert_fusion.2), channel_id=1, source_target_pairs={{0,3},{1,2},{2,1},{3,0},{4,7},{5,6},{6,5},{7,4},{8,11},{9,10},{10,... | collective-permute-start | bytes 2359304 | tf_op jit(solution)/shard_map/ppermute | solution.py:30
  136.2 26.0 %collective-permute-start.15 = (bf16[4,4,24,1024]{3,2,1,0:T(8,128)(2,1)S(1)}, bf16[4,4,24,1024]{3,2,1,0:T(8,128)(2,1)S(1)}, u32[]{:S(2)}, u32[]{:S(2)}) collective-permute-start(bf16[4,4,24,1024]{3,2,1,0:T(8,128)(2,1)S(1)} %pad_maximum_fusion.2.refs_0_), channel_id=1, source_target_pairs={{0,32},{1,33},{2,34},{3,35},{4,36},{5,37},{6,38},{7,39},{8,12},{9,... | collective-permute-start | bytes 2359304 | tf_op jit(solution)/shard_map/ppermute | solution.py:42
  138.0 25.1 %collective-permute-start.16 = (bf16[4,4,24,1024]{3,2,1,0:T(8,128)(2,1)S(1)}, bf16[4,4,24,1024]{3,2,1,0:T(8,128)(2,1)S(1)}, u32[]{:S(2)}, u32[]{:S(2)}) collective-permute-start(bf16[4,4,24,1024]{3,2,1,0:T(8,128)(2,1)S(1)} %pad_maximum_fusion.2.refs_0_), channel_id=1, source_target_pairs={{0,16},{1,17},{2,18},{3,19},{4,20},{5,21},{6,22},{7,23},{8,72},{9,... | collective-permute-start | bytes 2359304 | tf_op jit(solution)/shard_map/ppermute | solution.py:42
  154.9 19.5 %collective-permute-start.17 = (bf16[4,4,24,1024]{3,2,1,0:T(8,128)(2,1)S(1)}, bf16[4,4,24,1024]{3,2,1,0:T(8,128)(2,1)S(1)}, u32[]{:S(2)}, u32[]{:S(2)}) collective-permute-start(bf16[4,4,24,1024]{3,2,1,0:T(8,128)(2,1)S(1)} %pad_maximum_fusion.2.refs_0_), channel_id=1, source_target_pairs={{0,48},{1,49},{2,50},{3,51},{4,52},{5,53},{6,54},{7,55},{8,76},{9,... | collective-permute-start | bytes 2359304 | tf_op jit(solution)/shard_map/ppermute | solution.py:42
  157.0 19.0 %all-to-all-start.2 = ((bf16[16,24,1024]{2,1,0:T(8,128)(2,1)}), bf16[16,24,1024]{2,1,0:T(8,128)(2,1)}, u32[]{:S(2)}, u32[]{:S(2)}) async-start(bf16[16,24,1024]{2,1,0:T(8,128)(2,1)} %bitcast.100), calls=%async_computation.2 | async-start | bytes 1572864 | tf_op jit(solution)/shard_map/all_to_all | solution.py:174
  162.2 147.5 %reduce-scatter.2.cloned.1.call-start = ((), (), s32[]{:S(2)}) async-start(), calls=%async_computation.6 | async-start | bytes 2621440 | tf_op jit(solution)/shard_map/reduce_scatter | solution.py:192
  181.3 63.1 %collective-permute-start.23 = (bf16[1536,1024]{1,0:T(8,128)(2,1)S(1)}, bf16[1536,1024]{1,0:T(8,128)(2,1)}, u32[]{:S(2)}, u32[]{:S(2)}) collective-permute-start(bf16[1536,1024]{1,0:T(8,128)(2,1)S(1)} %bitcast.90), channel_id=1, source_target_pairs={{0,8},{1,9},{2,10},{3,11},{4,12},{5,13},{6,14},{7,15},{8,0},{9,1},... | collective-permute-start | bytes 9437192 | tf_op jit(solution)/shard_map/ppermute | solution.py:30
  192.0 24.3 %collective-permute-start.22 = (bf16[384,1024]{1,0:T(8,128)(2,1)}, bf16[384,1024]{1,0:T(8,128)(2,1)}, u32[]{:S(2)}, u32[]{:S(2)}) collective-permute-start(bf16[384,1024]{1,0:T(8,128)(2,1)} %collective-permute-done.19), channel_id=1, source_target_pairs={{0,1},{1,0},{2,3},{3,2},{4,5},{5,4},{6,7},{7,6},{8,9},{9,8},{10,11... | collective-permute-start | bytes 2359304 | tf_op jit(solution)/shard_map/ppermute | solution.py:30
  192.6 56.9 %collective-permute-start.24 = (bf16[384,1024]{1,0:T(8,128)(2,1)}, bf16[384,1024]{1,0:T(8,128)(2,1)}, u32[]{:S(2)}, u32[]{:S(2)}) collective-permute-start(bf16[384,1024]{1,0:T(8,128)(2,1)} %collective-permute-done.13), channel_id=1, source_target_pairs={{0,3},{1,2},{2,1},{3,0},{4,7},{5,6},{6,5},{7,4},{8,11},{9,10},{10,... | collective-permute-start | bytes 2359304 | tf_op jit(solution)/shard_map/ppermute | solution.py:30
  226.0 56.6 %all-to-all-start.3 = ((bf16[16,24,4096]{2,1,0:T(8,128)(2,1)}), bf16[16,24,4096]{2,1,0:T(8,128)(2,1)}, u32[]{:S(2)}, u32[]{:S(2)}) async-start(bf16[16,24,4096]{2,1,0:T(8,128)(2,1)} %bitcast.99), calls=%async_computation.3 | async-start | bytes 6291456 | tf_op jit(solution)/shard_map/all_to_all | solution.py:66
  252.8 50.2 %collective-permute-start.25 = (bf16[512,1024]{1,0:T(8,128)(2,1)S(1)}, bf16[512,1024]{1,0:T(8,128)(2,1)S(1)}, u32[]{:S(2)}, u32[]{:S(2)}) collective-permute-start(bf16[512,1024]{1,0:T(8,128)(2,1)S(1)} %get-tuple-element.62), channel_id=1, source_target_pairs={{0,4},{1,5},{2,6},{3,7},{4,0},{5,1},{6,2},{7,3},{8,12},{9,13},{10,... | collective-permute-start | bytes 3145736 | tf_op jit(solution)/shard_map/ppermute | solution.py:30
  284.1 24.1 %all-to-all-start.4 = ((bf16[16,8,24]{2,1,0:T(8,128)(2,1)}), bf16[16,8,24]{2,1,0:T(8,128)(2,1)}, u32[]{:S(2)}, u32[]{:S(2)}) async-start(bf16[16,8,24]{2,1,0:T(8,128)(2,1)} %copy.40), calls=%async_computation.4 | async-start | bytes 65536 | tf_op jit(solution)/shard_map/all_to_all | solution.py:203
  (29 other events, 286.3 us)
Sparse Core Ops, SparseCore 0:
  196.9 34.3 reduce-scatter.1
